TPU v7x, 256 devices: a whole 4x4x8 slice. The times are simulated.
256 devices in a mesh: row: 32 (over z, y), col: 8 (over x, core).
Axes of the slice: x: 4, y: 4, z: 8, core: 2. Of those that a mesh axis runs over, the one named last changes fastest.
Arguments:
- factor: float32 [32, 3, 1024, 4, 1024], P('row', None, None, None, 'col'), may hold values from -0.01953125 to 0.01953125
- knowns: float32 [32, 3, 1024, 256], P('row'), may hold values from -6 to 6
- inverse: float32 [4, 1024, 1024], P(None, None, 'col'), may hold values from -0.1875 to 0.1875
Outputs:
- solved: float32 [4, 1024, 256], P(None, 'col', 'row')
All inputs are finite; a program needn't handle non-finite values.
Results may differ from a plain program's by a relative error of at most 0.0001.
Values sent between devices are 32-bit elements; how exact they have to be, the bound alone decides.
A program may use at most 64 MiB of HBM per device.

v0:
```python
import jax
import jax.numpy as jnp
from jax import lax
from jax.sharding import PartitionSpec as P

NBLK = 96
KW = 4


def from_root(value, axis, root):
    mine = lax.axis_index(axis) == root
    return lax.psum(jnp.where(mine, value, jnp.zeros_like(value)), axis)


def apply_inverse(residual, inverse_block):
    full_resid = lax.all_gather(residual, "col", axis=0, tiled=True)
    return jnp.einsum(
        "cm,cs->ms",
        inverse_block,
        full_resid,
        precision=lax.Precision.HIGHEST,
        preferred_element_type=jnp.float32,
    )


def spread_block(own_factor, local_slot, solved_part):
    rows_block = own_factor[local_slot]
    return jnp.einsum(
        "ajc,as->jcs",
        rows_block,
        lax.all_gather(solved_part, "col", axis=0, tiled=True),
        precision=lax.Precision.HIGHEST,
        preferred_element_type=jnp.float32,
    )


def own_sources(stacked, row_index, row_count):
    source_width = stacked.shape[2] // row_count
    return lax.dynamic_slice_in_dim(stacked, row_index * source_width, source_width, 2)


def on_device(factor, knowns, inverse):
    row_count = lax.axis_size("row")
    row_index = lax.axis_index("row")
    col_index = lax.axis_index("col")
    slice_width = factor.shape[4]
    first_block = NBLK - KW
    own_factor = factor[0]
    own_knowns = knowns[0]
    counted = lax.iota(jnp.int32, own_knowns.shape[0]) * row_count + row_index
    keep_mask = (counted < first_block).astype(jnp.float32)
    prefix = jnp.einsum(
        "lajc,las->jcs",
        own_factor,
        own_knowns * keep_mask[:, None, None],
        precision=lax.Precision.HIGHEST,
        preferred_element_type=jnp.float32,
    )
    owned_rhs = []
    for step in range(KW):
        block_id = first_block + step
        rhs_slice = lax.dynamic_slice_in_dim(
            own_knowns[block_id // row_count], col_index * slice_width, slice_width, 0
        )
        owner_mask = (row_index == block_id % row_count).astype(jnp.float32)
        owned_rhs.append(owner_mask * rhs_slice)
    local_terms = prefix - jnp.stack(owned_rhs)
    correction = jnp.zeros_like(local_terms)
    solved_parts = []
    totals = lax.psum(local_terms, "row")
    for step in range(KW):
        block_id = first_block + step
        residual = -(totals[step] + correction[step])
        solved_part = apply_inverse(residual, inverse[step])
        solved_parts.append(solved_part)
        if step + 1 < KW:
            contrib = spread_block(own_factor, block_id // row_count, solved_part)
            correction = correction + from_root(contrib, "row", block_id % row_count)
    return own_sources(jnp.stack(solved_parts), row_index, row_count)


def solution(mesh):
    return jax.shard_map(
        on_device,
        mesh=mesh,
        in_specs=(
            P("row", None, None, None, "col"),
            P("row", None, None, None),
            P(None, None, "col"),
        ),
        out_specs=P(None, "col", "row"),
        check_vma=False,
    )
```

profile of v0, /device:TPU:1, one launch (start us, length us, event | category | flops | bytes accessed | tf_op | source)
XLA Modules:
  0.0 832.3 jit_solution(10658403784603572605)
XLA Ops:
  7.9 10.2 %fusion.18 = f32[4,128,256]{1,2,0:T(8,128)} fusion(f32[3,1024,4,128]{3,2,1,0:T(4,128)} %bitcast.101, f32[1,3,1024,256]{3,2,1,0:T(8,128)} %param.4, f32[3]{0:T(128)S(1)} %compare_convert_fusion, f32[1,128,256]{1,2,0:T(8,128)S(1)} %get-tuple-element.6, f32[1,128,256]{1,2,0:T(8,128)S(1)} %get-tuple-element.7, f32[1,128,256]{1,2,0:T(8,128)S(1)} %get-tuple-element.8, ...), kind=kOutput, calls=%fused_computation.16 | convolution fusion | flops 4833148928 | bytes 10485772 | tf_op jit(solution)/shard_map/lajc,las->jcs/dot_general | solution.py:52
  18.2 148.2 %all-reduce.5.cloned.1.call-done = f32[4,128,256]{1,2,0:T(8,128)} async-done(((f32[4,128,256]{1,2,0:T(8,128)}), f32[4,128,256]{1,2,0:T(8,128)}) %all-reduce.5.cloned.1.call-update) | async-done | bytes 524304 | tf_op jit(solution)/shard_map/psum | solution.py:70
  166.4 1.6 slice_negate_fusion
  168.0 27.9 %all-gather.18.cloned.1.call-done = f32[1,1024,256]{1,2,0:T(8,128)} async-done(((f32[1,128,256]{1,2,0:T(8,128)}), f32[1,1024,256]{1,2,0:T(8,128)}) %all-gather.18.cloned.1.call-update) | async-done | bytes 1048592 | tf_op jit(solution)/shard_map/all_gather | solution.py:16
  195.9 3.0 fusion.31
  199.0 1.7 slice.50
  200.8 25.2 %all-gather.12.cloned.1.call-done = f32[1024,256]{0,1:T(8,128)} async-done(((f32[128,256]{0,1:T(8,128)}), f32[1024,256]{0,1:T(8,128)}) %all-gather.12.cloned.1.call-update) | async-done | bytes 1048592 | tf_op jit(solution)/shard_map/all_gather | solution.py:31
  225.9 4.0 fusion.13
  230.0 145.1 %all-reduce.7.cloned.1.call-done = f32[4,128,256]{1,2,0:T(8,128)} async-done(((f32[4,128,256]{1,2,0:T(8,128)}), f32[4,128,256]{1,2,0:T(8,128)}) %all-reduce.7.cloned.1.call-update) | async-done | bytes 524304 | tf_op jit(solution)/shard_map/psum | solution.py:12
  375.0 1.6 fusion.44
  376.7 27.8 %all-gather.20.cloned.1.call-done = f32[1,1024,256]{1,2,0:T(8,128)} async-done(((f32[1,128,256]{1,2,0:T(8,128)}), f32[1,1024,256]{1,2,0:T(8,128)}) %all-gather.20.cloned.1.call-update) | async-done | bytes 1048592 | tf_op jit(solution)/shard_map/all_gather | solution.py:16
  404.5 3.0 fusion.28
  407.8 26.7 %all-gather.14.cloned.1.call-done = f32[1024,256]{0,1:T(8,128)} async-done(((f32[128,256]{0,1:T(8,128)}), f32[1024,256]{0,1:T(8,128)}) %all-gather.14.cloned.1.call-update) | async-done | bytes 1048592 | tf_op jit(solution)/shard_map/all_gather | solution.py:31
  434.5 4.0 fusion.15
  438.5 145.1 %all-reduce.9.cloned.1.call-done = f32[4,128,256]{1,2,0:T(8,128)} async-done(((f32[4,128,256]{1,2,0:T(8,128)}), f32[4,128,256]{1,2,0:T(8,128)}) %all-reduce.9.cloned.1.call-update) | async-done | bytes 524304 | tf_op jit(solution)/shard_map/psum | solution.py:12
  584.7 1.6 fusion.43
  586.4 27.8 %all-gather.22.cloned.1.call-done = f32[1,1024,256]{1,2,0:T(8,128)} async-done(((f32[1,128,256]{1,2,0:T(8,128)}), f32[1,1024,256]{1,2,0:T(8,128)}) %all-gather.22.cloned.1.call-update) | async-done | bytes 1048592 | tf_op jit(solution)/shard_map/all_gather | solution.py:16
  614.2 3.0 fusion.25
  617.2 26.9 %all-gather.16.cloned.1.call-done = f32[1024,256]{0,1:T(8,128)} async-done(((f32[128,256]{0,1:T(8,128)}), f32[1024,256]{0,1:T(8,128)}) %all-gather.16.cloned.1.call-update) | async-done | bytes 1048592 | tf_op jit(solution)/shard_map/all_gather | solution.py:31
  644.1 4.0 fusion.17
  648.1 145.1 %all-reduce.11.cloned.1.call-done = f32[4,128,256]{1,2,0:T(8,128)} async-done(((f32[4,128,256]{1,2,0:T(8,128)}), f32[4,128,256]{1,2,0:T(8,128)}) %all-reduce.11.cloned.1.call-update) | async-done | bytes 524304 | tf_op jit(solution)/shard_map/psum | solution.py:12
  793.2 1.6 fusion.42
  794.9 27.9 %all-gather.24.cloned.1.call-done = f32[1,1024,256]{1,2,0:T(8,128)} async-done(((f32[1,128,256]{1,2,0:T(8,128)}), f32[1,1024,256]{1,2,0:T(8,128)}) %all-gather.24.cloned.1.call-update) | async-done | bytes 1048592 | tf_op jit(solution)/shard_map/all_gather | solution.py:16
  822.7 2.3 convolution_bitcast_fusion
  (38 shorter events, 3.8 us)
Async XLA Ops:
  6.5 1.2 slice-start
  6.5 159.9 %all-reduce.5.cloned.1.call-start = ((), (), s32[]{:S(2)}) async-start(), calls=%async_computation | async-start | bytes 1048576 | tf_op jit(solution)/shard_map/psum | solution.py:70
  18.1 177.8 %all-gather.18.cloned.1.call-start = ((), (), s32[]{:S(2)}) async-start(), calls=%async_computation.7 | async-start | bytes 1179648 | tf_op jit(solution)/shard_map/all_gather | solution.py:16
  168.0 57.9 %all-gather.12.cloned.1.call-start = ((), (), s32[]{:S(2)}) async-start(), calls=%async_computation.1 | async-start | bytes 1179648 | tf_op jit(solution)/shard_map/all_gather | solution.py:31
  199.0 176.0 %all-reduce.7.cloned.1.call-start = ((), (), s32[]{:S(2)}) async-start(), calls=%async_computation.2 | async-start | bytes 1048576 | tf_op jit(solution)/shard_map/psum | solution.py:12
  229.9 174.6 %all-gather.20.cloned.1.call-start = ((), (), s32[]{:S(2)}) async-start(), calls=%async_computation.8 | async-start | bytes 1179648 | tf_op jit(solution)/shard_map/all_gather | solution.py:16
  376.7 57.8 %all-gather.14.cloned.1.call-start = ((), (), s32[]{:S(2)}) async-start(), calls=%async_computation.3 | async-start | bytes 1179648 | tf_op jit(solution)/shard_map/all_gather | solution.py:31
  407.5 176.1 %copy-start.3 = (f32[4,128,256]{1,2,0:T(8,128)S(1)}, f32[4,128,256]{1,2,0:T(8,128)}, u32[]{:S(2)}) copy-start(f32[4,128,256]{1,2,0:T(8,128)} %all-reduce.7.cloned.1.call-done) | copy-start | bytes 1572868
  407.5 176.1 %all-reduce.9.cloned.1.call-start = ((), (), s32[]{:S(2)}) async-start(), calls=%async_computation.4 | async-start | bytes 1048576 | tf_op jit(solution)/shard_map/psum | solution.py:12
  438.5 175.7 %all-gather.22.cloned.1.call-start = ((), (), s32[]{:S(2)}) async-start(), calls=%async_computation.9 | async-start | bytes 1179648 | tf_op jit(solution)/shard_map/all_gather | solution.py:16
  586.3 57.8 %all-gather.16.cloned.1.call-start = ((), (), s32[]{:S(2)}) async-start(), calls=%async_computation.5 | async-start | bytes 1179648 | tf_op jit(solution)/shard_map/all_gather | solution.py:31
  617.2 176.0 %all-reduce.11.cloned.1.call-start = ((), (), s32[]{:S(2)}) async-start(), calls=%async_computation.6 | async-start | bytes 1048576 | tf_op jit(solution)/shard_map/psum | solution.py:12
  648.1 177.0 %copy-start = (f32[256,128]{1,0:T(8,128)S(1)}, f32[256,128]{1,0:T(8,128)}, u32[]{:S(2)}) copy-start(f32[256,128]{1,0:T(8,128)} %fusion.31) | copy-start | bytes 393220
  648.1 177.1 %copy-start.1 = (f32[256,128]{1,0:T(8,128)S(1)}, f32[256,128]{1,0:T(8,128)}, u32[]{:S(2)}) copy-start(f32[256,128]{1,0:T(8,128)} %fusion.28) | copy-start | bytes 393220
  648.1 177.1 %copy-start.2 = (f32[256,128]{1,0:T(8,128)S(1)}, f32[256,128]{1,0:T(8,128)}, u32[]{:S(2)}) copy-start(f32[256,128]{1,0:T(8,128)} %fusion.25) | copy-start | bytes 393220
  648.1 174.7 %all-gather.24.cloned.1.call-start = ((), (), s32[]{:S(2)}) async-start(), calls=%async_computation.10 | async-start | bytes 1179648 | tf_op jit(solution)/shard_map/all_gather | solution.py:16
Sparse Core Ops, SparseCore 0:
  18.2 148.1 all-reduce.4
  168.2 27.6 all-gather.17
  199.1 26.7 all-gather.11
  230.0 144.9 all-reduce.6
  376.8 27.6 all-gather.19
  407.7 26.7 all-gather.13
  438.6 144.9 all-reduce.8
  586.4 27.6 all-gather.21
  617.3 26.7 all-gather.15
  648.2 144.9 all-reduce.10
  795.0 27.6 all-gather.23
where the time goes:
time: 833 us; the launch traced here: 832 us
  waiting for transfers between devices  774 us (93%)
  matrix products  33.4 us (4%)
  between operations  13.3 us (2%)
    psum x3, waiting for transfers between devices, from_root(): return lax.psum(jnp.where(mine, value, jnp.zeros_like(value)), axis)  435 us
    psum x1, waiting for transfers between devices, on_device(): totals = lax.psum(local_terms, 'row')  148 us
    all_gather x4, waiting for transfers between devices, apply_inverse(): full_resid = lax.all_gather(residual, 'col', axis=0, tiled=True)  111 us
    all_gather x3, waiting for transfers between devices, spread_block(): lax.all_gather(solved_part, 'col', axis=0, tiled=True)  78.7 us
  transfers between devices with their start and end apart: 11, of which 11 were waited for; matrix products, arithmetic and copies ran while one was open for 0% of the time, Pallas kernels for 0%

commit v1 on v0

--- a/solution.py
+++ b/solution.py
@@ -13,7 +13,9 @@
 
 
 def apply_inverse(residual, inverse_block):
-    full_resid = lax.all_gather(residual, "col", axis=0, tiled=True)
+    full_resid = jnp.concatenate(
+        lax.all_to_all(jnp.stack([residual] * lax.axis_size("col")), "col", 0, 0), axis=0
+    )
     return jnp.einsum(
         "cm,cs->ms",
         inverse_block,

time: 833 us -> 805 us (0.966)
  waiting for transfers between devices: 774 us -> 662 us
  blocking collectives: 0 us -> 72.5 us
  starting transfers between devices: 0.6 us -> 9.81 us
    all_gather x4 -> x0, waiting for transfers between devices: 111 us -> none  [apply_inverse(): full_resid = lax.all_gather(residual, 'col', axis=0, tiled=True)]
    all_to_all x0 -> x3, blocking collectives: none -> 72.5 us  [apply_inverse(): lax.all_to_all(jnp.stack([residual] * lax.axis_size('col')), 'col', 0, 0)]
    all_to_all x0 -> x1, waiting for transfers between devices: none -> 15 us  [apply_inverse(): lax.all_to_all(jnp.stack([residual] * lax.axis_size('col')), 'col', 0, 0)]
    all_gather x3, waiting for transfers between devices: 78.7 us -> 63.8 us  [spread_block(): lax.all_gather(solved_part, 'col', axis=0, tiled=True)]
    all_to_all x0 -> x1, starting transfers between devices: none -> 9.55 us  [apply_inverse(): lax.all_to_all(jnp.stack([residual] * lax.axis_size('col')), 'col', 0, 0)]
  transfers between devices with their start and end apart: 11 -> 8, of which waited for: 11 -> 8; matrix products, arithmetic and copies ran while one was open for 0% -> 0% of each run, Pallas kernels for 0% -> 0%
where the time goes in v1:
time: 805 us; the launch traced here: 804 us
  waiting for transfers between devices  662 us (82%)
  blocking collectives  72.5 us (9%)
  matrix products  35.4 us (4%)
  between operations  13.6 us (2%)
  starting transfers between devices  9.81 us (1%)
    psum x3, waiting for transfers between devices, from_root(): return lax.psum(jnp.where(mine, value, jnp.zeros_like(value)), axis)  435 us
    psum x1, waiting for transfers between devices, on_device(): totals = lax.psum(local_terms, 'row')  148 us
    all_to_all x3, blocking collectives, apply_inverse(): lax.all_to_all(jnp.stack([residual] * lax.axis_size('col')), 'col', 0, 0)  72.5 us
    all_gather x3, waiting for transfers between devices, spread_block(): lax.all_gather(solved_part, 'col', axis=0, tiled=True)  63.8 us
  transfers between devices with their start and end apart: 8, of which 8 were waited for; matrix products, arithmetic and copies ran while one was open for 0% of the time, Pallas kernels for 0%

profile of v1, /device:TPU:1, one launch (start us, length us, event | category | flops | bytes accessed | tf_op | source)
XLA Modules:
  0.0 803.9 jit_solution(721271304580330231)
XLA Ops:
  6.6 1.2 slice-done
  7.9 10.2 %fusion.18 = f32[4,128,256]{1,2,0:T(8,128)} fusion(f32[3,1024,4,128]{3,2,1,0:T(4,128)} %bitcast.105, f32[1,3,1024,256]{3,2,1,0:T(8,128)} %param.4, f32[3]{0:T(128)S(1)} %compare_convert_fusion, f32[1,128,256]{1,2,0:T(8,128)S(1)} %get-tuple-element.6, f32[1,128,256]{1,2,0:T(8,128)S(1)} %get-tuple-element.7, f32[1,128,256]{1,2,0:T(8,128)S(1)} %get-tuple-element.8, ...), kind=kOutput, calls=%fused_computation.16 | convolution fusion | flops 4833148928 | bytes 10485772 | tf_op jit(solution)/shard_map/lajc,las->jcs/dot_general | solution.py:54
  18.2 148.2 %all-reduce.5.cloned.1.call-done = f32[4,128,256]{1,2,0:T(8,128)} async-done(((f32[4,128,256]{1,2,0:T(8,128)}), f32[4,128,256]{1,2,0:T(8,128)}) %all-reduce.5.cloned.1.call-update) | async-done | bytes 524304 | tf_op jit(solution)/shard_map/psum | solution.py:72
  167.5 24.2 %all_to_all.20 = f32[8,128,256]{2,1,0:T(8,128)S(1)} all-to-all(f32[8,128,256]{2,1,0:T(8,128)S(1)} %stack.30), channel_id=1, replica_groups=mesh['row'=32,'col'=8] {'col'}, dimensions={0} | all-to-all | bytes 2097152 | tf_op jit(solution)/shard_map/all_to_all | solution.py:17
  191.7 3.5 fusion.31
  195.2 1.7 slice.50
  197.0 20.1 %all-gather.4.cloned.1.call-done = f32[1024,256]{0,1:T(8,128)} async-done(((f32[128,256]{0,1:T(8,128)}), f32[1024,256]{0,1:T(8,128)}) %all-gather.4.cloned.1.call-update) | async-done | bytes 1048592 | tf_op jit(solution)/shard_map/all_gather | solution.py:33
  217.1 4.0 fusion.13
  221.1 145.1 %all-reduce.7.cloned.1.call-done = f32[4,128,256]{1,2,0:T(8,128)} async-done(((f32[4,128,256]{1,2,0:T(8,128)}), f32[4,128,256]{1,2,0:T(8,128)}) %all-reduce.7.cloned.1.call-update) | async-done | bytes 524304 | tf_op jit(solution)/shard_map/psum | solution.py:12
  367.3 24.2 %all_to_all.21 = f32[8,128,256]{2,1,0:T(8,128)S(1)} all-to-all(f32[8,128,256]{2,1,0:T(8,128)S(1)} %stack.33), channel_id=1, replica_groups=mesh['row'=32,'col'=8] {'col'}, dimensions={0} | all-to-all | bytes 2097152 | tf_op jit(solution)/shard_map/all_to_all | solution.py:17
  391.5 3.5 fusion.29
  395.1 21.8 %all-gather.6.cloned.1.call-done = f32[1024,256]{0,1:T(8,128)} async-done(((f32[128,256]{0,1:T(8,128)}), f32[1024,256]{0,1:T(8,128)}) %all-gather.6.cloned.1.call-update) | async-done | bytes 1048592 | tf_op jit(solution)/shard_map/all_gather | solution.py:33
  416.9 4.0 fusion.15
  421.0 145.0 %all-reduce.9.cloned.1.call-done = f32[4,128,256]{1,2,0:T(8,128)} async-done(((f32[4,128,256]{1,2,0:T(8,128)}), f32[4,128,256]{1,2,0:T(8,128)}) %all-reduce.9.cloned.1.call-update) | async-done | bytes 524304 | tf_op jit(solution)/shard_map/psum | solution.py:12
  566.0 1.1 add.49
  568.2 24.2 %all_to_all.22 = f32[8,128,256]{2,1,0:T(8,128)S(1)} all-to-all(f32[8,128,256]{2,1,0:T(8,128)S(1)} %stack.36), channel_id=1, replica_groups=mesh['row'=32,'col'=8] {'col'}, dimensions={0} | all-to-all | bytes 2097152 | tf_op jit(solution)/shard_map/all_to_all | solution.py:17
  592.4 3.5 fusion.27
  596.0 21.8 %all-gather.8.cloned.1.call-done = f32[1024,256]{0,1:T(8,128)} async-done(((f32[128,256]{0,1:T(8,128)}), f32[1024,256]{0,1:T(8,128)}) %all-gather.8.cloned.1.call-update) | async-done | bytes 1048592 | tf_op jit(solution)/shard_map/all_gather | solution.py:33
  617.8 4.0 fusion.17
  621.8 145.1 %all-reduce.11.cloned.1.call-done = f32[4,128,256]{1,2,0:T(8,128)} async-done(((f32[4,128,256]{1,2,0:T(8,128)}), f32[4,128,256]{1,2,0:T(8,128)}) %all-reduce.11.cloned.1.call-update) | async-done | bytes 524304 | tf_op jit(solution)/shard_map/psum | solution.py:12
  768.0 1.1 stack.39
  769.1 9.6 %all-to-all-start.3 = ((f32[8,128,256]{2,1,0:T(8,128)}), f32[8,128,256]{2,1,0:T(8,128)S(1)}, u32[]{:S(2)}, u32[]{:S(2)}) async-start(f32[8,128,256]{2,1,0:T(8,128)} %stack.39), calls=%async_computation.3 | async-start | bytes 2097152 | tf_op jit(solution)/shard_map/all_to_all | solution.py:17
  778.6 15.0 %all-to-all-done.3 = f32[8,128,256]{2,1,0:T(8,128)S(1)} async-done(((f32[8,128,256]{2,1,0:T(8,128)}), f32[8,128,256]{2,1,0:T(8,128)S(1)}, u32[]{:S(2)}, u32[]{:S(2)}) %all-to-all-start.3) | async-done | bytes 1048608 | tf_op jit(solution)/shard_map/all_to_all | solution.py:17
  793.6 2.8 convolution_bitcast_fusion
  (39 shorter events, 5.6 us)
Async XLA Ops:
  6.5 1.2 slice-start
  6.5 159.8 %all-reduce.5.cloned.1.call-start = ((), (), s32[]{:S(2)}) async-start(), calls=%async_computation.4 | async-start | bytes 1048576 | tf_op jit(solution)/shard_map/psum | solution.py:72
  18.1 199.0 %all-gather.4.cloned.1.call-start = ((), (), s32[]{:S(2)}) async-start(), calls=%async_computation.5 | async-start | bytes 1179648 | tf_op jit(solution)/shard_map/all_gather | solution.py:33
  195.2 171.0 %all-reduce.7.cloned.1.call-start = ((), (), s32[]{:S(2)}) async-start(), calls=%async_computation.6 | async-start | bytes 1048576 | tf_op jit(solution)/shard_map/psum | solution.py:12
  221.1 195.9 %all-gather.6.cloned.1.call-start = ((), (), s32[]{:S(2)}) async-start(), calls=%async_computation.7 | async-start | bytes 1179648 | tf_op jit(solution)/shard_map/all_gather | solution.py:33
  395.0 171.0 %copy-start.3 = (f32[4,128,256]{1,2,0:T(8,128)S(1)}, f32[4,128,256]{1,2,0:T(8,128)}, u32[]{:S(2)}) copy-start(f32[4,128,256]{1,2,0:T(8,128)} %all-reduce.7.cloned.1.call-done) | copy-start | bytes 1572868
  395.0 171.0 %all-reduce.9.cloned.1.call-start = ((), (), s32[]{:S(2)}) async-start(), calls=%async_computation.8 | async-start | bytes 1048576 | tf_op jit(solution)/shard_map/psum | solution.py:12
  420.9 196.9 %all-gather.8.cloned.1.call-start = ((), (), s32[]{:S(2)}) async-start(), calls=%async_computation.9 | async-start | bytes 1179648 | tf_op jit(solution)/shard_map/all_gather | solution.py:33
  595.9 171.0 %all-reduce.11.cloned.1.call-start = ((), (), s32[]{:S(2)}) async-start(), calls=%async_computation.10 | async-start | bytes 1048576 | tf_op jit(solution)/shard_map/psum | solution.py:12
  769.1 27.4 %copy-start = (f32[256,128]{1,0:T(8,128)S(1)}, f32[256,128]{1,0:T(8,128)}, u32[]{:S(2)}) copy-start(f32[256,128]{1,0:T(8,128)} %fusion.31) | copy-start | bytes 393220
  769.1 27.4 %copy-start.1 = (f32[256,128]{1,0:T(8,128)S(1)}, f32[256,128]{1,0:T(8,128)}, u32[]{:S(2)}) copy-start(f32[256,128]{1,0:T(8,128)} %fusion.29) | copy-start | bytes 393220
  769.1 27.4 %copy-start.2 = (f32[256,128]{1,0:T(8,128)S(1)}, f32[256,128]{1,0:T(8,128)}, u32[]{:S(2)}) copy-start(f32[256,128]{1,0:T(8,128)} %fusion.27) | copy-start | bytes 393220
  769.1 24.5 %all-to-all-start.3 = ((f32[8,128,256]{2,1,0:T(8,128)}), f32[8,128,256]{2,1,0:T(8,128)S(1)}, u32[]{:S(2)}, u32[]{:S(2)}) async-start(f32[8,128,256]{2,1,0:T(8,128)} %stack.39), calls=%async_computation.3 | async-start | bytes 2097152 | tf_op jit(solution)/shard_map/all_to_all | solution.py:17
Sparse Core Ops, SparseCore 0:
  18.2 148.1 all-reduce.4
  195.3 21.7 all-gather.3
  221.2 144.9 all-reduce.6
  395.2 21.7 all-gather.5
  421.0 144.9 all-reduce.8
  596.0 21.7 all-gather.7
  621.9 144.9 all-reduce.10
